TPU v7x, 32 devices: a whole 2x2x4 slice. The times are simulated.
32 devices in a mesh: spec: 8 (over z, y), wave: 4 (over x, core).
Axes of the slice: x: 2, y: 2, z: 4, core: 2. Of those that a mesh axis runs over, the one named last changes fastest.
Arguments:
- observed_flux: bfloat16 [2048, 2048], P('spec', 'wave'), may hold values from -6 to 6
- continuum_coeffs: bfloat16 [2048, 16], P('spec'), may hold values from -6 to 6
- continuum_basis: bfloat16 [16, 2048], P(None, 'wave'), may hold values from -1.5 to 1.5
- centres: int32 [2048, 16], P('spec', 'wave'), may hold values from 0 to 2047, as said below
- line_index: int32 [2048, 16], P('spec', 'wave'), may hold values from 0 to 31
- column_factor: float32 [2048, 16], P('spec', 'wave'), may hold values from 0.3 to 3
- wing_width: int32 [2048], P('spec'), may hold values from 8 to 32, as said below
- line_strength: float32 [32], replicated, may hold values from 0.2 to 2
- line_widths: float32 [32], replicated, may hold values from 1 to 6
- sketch_matrix: bfloat16 [2048, 512], P('wave'), may hold values from -0.125 to 0.125
Outputs:
- residual: bfloat16 [2048, 2048], P('spec', 'wave')
- rfactor: float32 [512, 512], replicated
Inputs may be any that keep to these rules, and one draw needn't show every extreme that they name: The absorbers in columns k * 4 to (k + 1) * 4 - 1 have centres in pixels k * 512 to (k + 1) * 512 - 1; spectrum 0 has absorbers at pixel 0 and at pixel 2048 - 1. `wing_width`: spectrum 0 has the largest half-width.
All inputs are finite; a program needn't handle non-finite values.
Results may differ from a plain program's by a relative error of at most 0.0026.
Values sent between devices are 32-bit elements; how exact they have to be, the bound alone decides.
No kernel may reach another device: no remote copies, remote signals or barrier semaphores. Data moves between devices by JAX's collectives and lax.ppermute only.
A program may use at most 64 MiB of HBM per device.

v0:
```python
import jax
import jax.numpy as jnp
from jax import lax
from jax.sharding import PartitionSpec as P

WING = 32
voigt_mix = 0.5
log_two = 0.6931471805599453


def extended_2(block, sides, width):
    for axis, dim in sides:
        count = lax.axis_size(axis)
        forward = [(i, i + 1) for i in range(count - 1)]
        backward = [(target, source) for source, target in forward]
        low = lax.ppermute(
            lax.slice_in_dim(block, block.shape[dim] - width, None, axis=dim), axis, forward
        )
        high = lax.ppermute(lax.slice_in_dim(block, 0, width, axis=dim), axis, backward)
        block = jnp.concatenate([low, block, high], axis=dim)
    return block


def profile(offset, amplitude, inverse_width, wing_limit):
    scaled = offset * inverse_width
    values = amplitude * (
        voigt_mix / (1.0 + scaled * scaled)
        + (1.0 - voigt_mix) * jnp.exp(-log_two * scaled * scaled)
    )
    return jnp.where(jnp.abs(offset) <= wing_limit, values, 0.0)


def windowed_depth(centre_int, amplitude, inverse_width, wing_limit, anchor, width):
    pixels = anchor + jnp.arange(width, dtype=jnp.int32)
    offset_int = pixels[None, None, :] - centre_int[:, :, None]
    offset_float = offset_int.astype(jnp.float32)
    values = profile(
        offset_float, amplitude[:, :, None], inverse_width[:, :, None], wing_limit[:, :, None]
    )
    return jnp.sum(values, axis=1)


def shards(
    observed_flux,
    continuum_coeffs,
    continuum_basis,
    centres,
    line_index,
    column_factor,
    wing_width,
    line_strength,
    line_widths,
    sketch_matrix,
):
    spectra, pix_local = observed_flux.shape
    first_pixel = lax.axis_index("wave") * pix_local
    onehot = (
        line_index[:, :, None] == jnp.arange(line_strength.shape[0], dtype=jnp.int32)[None, None, :]
    ).astype(jnp.float32)
    amplitude = column_factor * jnp.sum(onehot * line_strength, axis=2)
    inverse_width = 1.0 / jnp.sum(onehot * line_widths, axis=2)
    wing_limit = wing_width.astype(jnp.float32)[:, None]
    extended = windowed_depth(
        centres, amplitude, inverse_width, wing_limit, first_pixel - WING, pix_local + 2 * WING
    )
    outgoing = jnp.concatenate([extended[:, :WING], extended[:, -WING:]], axis=1)
    padded_rims = extended_2(outgoing, (("wave", 1),), WING)
    optical_depth = extended[:, WING:-WING]
    optical_depth = optical_depth.at[:, :WING].add(padded_rims[:, :WING])
    optical_depth = optical_depth.at[:, -WING:].add(padded_rims[:, 3 * WING :])
    continuum = jnp.dot(continuum_coeffs, continuum_basis, preferred_element_type=jnp.float32)
    residual = (observed_flux.astype(jnp.float32) - continuum * jnp.exp(-optical_depth)).astype(
        jnp.bfloat16
    )
    spectra_total = spectra * lax.axis_size("spec")
    partial_sketch = jnp.dot(residual, sketch_matrix, preferred_element_type=jnp.float32)
    sketch = lax.psum(partial_sketch, "wave")
    local_gram = jnp.dot(
        sketch.T, sketch, precision=lax.Precision.HIGHEST, preferred_element_type=jnp.float32
    )
    gram_matrix = lax.psum(local_gram, "spec")
    gram_matrix = gram_matrix / spectra_total
    rfactor = jnp.linalg.cholesky(gram_matrix).T
    return (residual, rfactor)


def solution(mesh):
    return jax.shard_map(
        shards,
        mesh=mesh,
        in_specs=(
            P("spec", "wave"),
            P("spec", None),
            P(None, "wave"),
            P("spec", "wave"),
            P("spec", "wave"),
            P("spec", "wave"),
            P("spec"),
            P(),
            P(),
            P("wave", None),
        ),
        out_specs=(P("spec", "wave"), P()),
        check_vma=False,
    )
```

profile of v0, /device:TPU:0, one launch (start us, length us, event | category | flops | bytes accessed | tf_op | source)
XLA Modules:
  0.0 237.7 jit_solution(6965424051535711169)
XLA Ops:
  7.2 0.7 convert_element_type.15
  8.0 0.8 select_reduce_fusion.1
  8.8 0.7 mul.59
  9.5 2.2 fusion.5
  11.8 2.4 collective-permute-start
  14.3 1.3 collective-permute-start.1
  16.0 0.6 compare_reduce_fusion.4
  16.6 0.7 add_select_fusion
  17.3 1.1 scatter-add.6
  18.4 1.3 collective-permute-done.1
  19.7 0.9 scatter-add.9
  20.9 1.1 fusion.19
  22.3 36.6 %all-reduce.4.cloned.1.call-done = f32[256,512]{1,0:T(8,128)} async-done(((f32[256,512]{1,0:T(8,128)}), f32[256,512]{1,0:T(8,128)}) %all-reduce.4.cloned.1.call-update) | async-done | bytes 524304 | tf_op jit(solution)/shard_map/psum | solution.py:77
  58.9 3.2 %fusion.20 = f32[512,512]{0,1:T(8,128)} fusion(f32[256,512]{1,0:T(8,128)} %all-reduce.4.cloned.1.call-done), kind=kOutput, calls=%fused_computation.57 | convolution fusion | flops 805306368 | bytes 1572864 | tf_op jit(solution)/shard_map/dot_general | solution.py:78
  62.2 78.9 %all-reduce.6.cloned.1.call-done = f32[512,512]{0,1:T(8,128)} async-done(((f32[512,512]{0,1:T(8,128)}), f32[512,512]{0,1:T(8,128)}) %all-reduce.6.cloned.1.call-update) | async-done | bytes 1048592 | tf_op jit(solution)/shard_map/psum | solution.py:81
  141.0 2.3 broadcast_multiply_fusion
  143.3 1.6 copy.23
  145.3 1.0 copy-done.2
  146.2 11.7 %cholesky.104 = f32[128,128]{1,0:T(8,128)S(1)} custom-call(f32[128,128]{1,0:T(8,128)S(1)} %cholesky.266), custom_call_target="Cholesky" | custom-call | tf_op jit(solution)/shard_map/jit(cholesky)/cholesky | solution.py:83
  158.0 9.8 %custom-call.27 = f32[1,128,128]{1,2,0:T(8,128)S(1)} custom-call(f32[1,128,128]{2,1,0:T(8,128)S(1)} %get-tuple-element.44), custom_call_target="InvertDiagBlocksLowerTriangular" | custom-call | tf_op jit(solution)/shard_map/jit(cholesky)/cholesky | solution.py:83
  168.3 0.3 convolution_subtract_fusion
  168.6 11.8 %cholesky.217 = f32[128,128]{1,0:T(8,128)S(1)} custom-call(f32[128,128]{1,0:T(8,128)S(1)} %cholesky.270), custom_call_target="Cholesky" | custom-call | tf_op jit(solution)/shard_map/jit(cholesky)/cholesky | solution.py:83
  180.5 9.8 %custom-call.28 = f32[1,128,128]{1,2,0:T(8,128)S(1)} custom-call(f32[1,128,128]{2,1,0:T(8,128)S(1)} %get-tuple-element.41), custom_call_target="InvertDiagBlocksLowerTriangular" | custom-call | tf_op jit(solution)/shard_map/jit(cholesky)/cholesky | solution.py:83
  190.6 0.4 convolution_subtract_fusion.1
  191.0 11.7 %cholesky.238 = f32[128,128]{1,0:T(8,128)S(1)} custom-call(f32[128,128]{1,0:T(8,128)S(1)} %cholesky.275), custom_call_target="Cholesky" | custom-call | tf_op jit(solution)/shard_map/jit(cholesky)/cholesky | solution.py:83
  202.7 0.7 compare_reduce_fusion.1
  203.4 9.8 %custom-call.29 = f32[1,128,128]{1,2,0:T(8,128)S(1)} custom-call(f32[1,128,128]{2,1,0:T(8,128)S(1)} %get-tuple-element.38), custom_call_target="InvertDiagBlocksLowerTriangular" | custom-call | tf_op jit(solution)/shard_map/jit(cholesky)/cholesky | solution.py:83
  213.5 0.4 convolution_subtract_fusion.2
  213.9 11.7 %cholesky.255 = f32[128,128]{1,0:T(8,128)S(1)} custom-call(f32[128,128]{1,0:T(8,128)S(1)} %convolution_subtract_fusion.2), custom_call_target="Cholesky" | custom-call | tf_op jit(solution)/shard_map/jit(cholesky)/cholesky | solution.py:83
  225.6 0.6 compare_reduce_fusion
  226.2 0.7 compare_reduce_fusion.2
  229.6 1.3 copy.24
  (43 shorter events, 2.7 us)
Async XLA Ops:
  7.2 13.8 %copy-start = (bf16[512,512]{1,0:T(8,128)(2,1)S(1)}, bf16[512,512]{1,0:T(8,128)(2,1)}, u32[]{:S(2)}) copy-start(bf16[512,512]{1,0:T(8,128)(2,1)} %param.23) | copy-start | bytes 1572868
  7.2 51.8 %all-reduce.4.cloned.1.call-start = ((), (), s32[]{:S(2)}) async-start(), calls=%async_computation | async-start | bytes 1048576 | tf_op jit(solution)/shard_map/psum | solution.py:77
  11.8 4.8 %collective-permute-start = (f32[256,32]{1,0:T(8,128)S(1)}, f32[256,32]{1,0:T(8,128)S(1)}, u32[]{:S(2)}, u32[]{:S(2)}) collective-permute-start(f32[256,32]{1,0:T(8,128)S(1)} %copy.28), channel_id=1, source_target_pairs={{0,1},{1,2},{2,3},{4,5},{5,6},{6,7},{8,9},{9,10},{10,11},{12,13},{... | collective-permute-start | bytes 98312 | tf_op jit(solution)/shard_map/ppermute | solution.py:16
  14.3 5.3 %collective-permute-start.1 = (f32[256,32]{1,0:T(8,128)S(1)}, f32[256,32]{1,0:T(8,128)S(1)}, u32[]{:S(2)}, u32[]{:S(2)}) collective-permute-start(f32[256,32]{1,0:T(8,128)S(1)} %copy.29), channel_id=1, source_target_pairs={{1,0},{2,1},{3,2},{5,4},{6,5},{7,6},{9,8},{10,9},{11,10},{13,12},{... | collective-permute-start | bytes 98312 | tf_op jit(solution)/shard_map/ppermute | solution.py:19
  15.6 5.0 %copy-start.5 = (bf16[256,512]{1,0:T(8,128)(2,1)S(1)}, bf16[256,512]{1,0:T(8,128)(2,1)}, u32[]{:S(2)}) copy-start(bf16[256,512]{1,0:T(8,128)(2,1)} %param.14) | copy-start | bytes 786436
  15.7 5.0 %copy-start.6 = (bf16[16,512]{1,0:T(8,128)(2,1)S(1)}, bf16[16,512]{1,0:T(8,128)(2,1)}, u32[]{:S(2)}) copy-start(bf16[16,512]{1,0:T(8,128)(2,1)} %param.16) | copy-start | bytes 49156
  15.7 5.0 %copy-start.7 = (bf16[256,16]{0,1:T(8,128)(2,1)S(1)}, bf16[256,16]{0,1:T(8,128)(2,1)}, u32[]{:S(2)}) copy-start(bf16[256,16]{0,1:T(8,128)(2,1)} %param.15) | copy-start | bytes 24580
  20.9 41.2 %copy-start.4 = (bf16[256,512]{1,0:T(8,128)(2,1)}, bf16[256,512]{1,0:T(8,128)(2,1)S(1)}, u32[]{:S(2)}) copy-start(bf16[256,512]{1,0:T(8,128)(2,1)S(1)} %subtract_convert_fusion) | copy-start | bytes 786436
  22.1 119.0 %all-reduce.6.cloned.1.call-start = ((), (), s32[]{:S(2)}) async-start(), calls=%async_computation.1 | async-start | bytes 2097152 | tf_op jit(solution)/shard_map/psum | solution.py:81
  143.3 1.7 copy-start.1
  145.2 1.0 copy-start.2
  146.2 21.7 %copy-start.3 = (f32[512,512]{1,0:T(8,128)S(1)}, f32[512,512]{1,0:T(8,128)}, u32[]{:S(2)}) copy-start(f32[512,512]{1,0:T(8,128)} %copy-done.2) | copy-start | bytes 3145732
Sparse Core Ops, SparseCore 0:
  22.2 36.7 all-reduce.3
  63.0 77.9 all-reduce.5
where the time goes:
time: 238 us
  waiting for transfers between devices  117 us (49%)
  other arithmetic  87.1 us (37%)
  between operations  16.9 us (7%)
  local copies, waits for them, and re-layouts  6.6 us (3%)
  matrix products  6.44 us (3%)
  starting transfers between devices  3.91 us (2%)
    psum x1, waiting for transfers between devices, shards(): gram_matrix = lax.psum(local_gram, 'spec')  78.9 us
    another operation x14, other arithmetic, shards(): rfactor = jnp.linalg.cholesky(gram_matrix).T  78.6 us
    psum x1, waiting for transfers between devices, shards(): sketch = lax.psum(partial_sketch, 'wave')  36.6 us
  transfers between devices with their start and end apart: 4, of which 3 were waited for; matrix products, arithmetic and copies ran while one was open for 1% of the time, Pallas kernels for 0%

commit v1 on v0

--- a/solution.py
+++ b/solution.py
@@ -78,7 +78,11 @@
     local_gram = jnp.dot(
         sketch.T, sketch, precision=lax.Precision.HIGHEST, preferred_element_type=jnp.float32
     )
-    gram_matrix = lax.psum(local_gram, "spec")
+    gram_matrix = local_gram
+    for hop in (1, 2, 4):
+        gram_matrix = gram_matrix + lax.ppermute(
+            gram_matrix, "spec", [(dev, dev ^ hop) for dev in range(8)]
+        )
     gram_matrix = gram_matrix / spectra_total
     rfactor = jnp.linalg.cholesky(gram_matrix).T
     return (residual, rfactor)

time: 238 us -> 248 us (1.042)
  waiting for transfers between devices: 117 us -> 124 us
  starting transfers between devices: 3.91 us -> 9.8 us
    ppermute x0 -> x3, waiting for transfers between devices: none -> 86.4 us  [shards(): lax.ppermute(gram_matrix, 'spec', [(dev, dev ^ hop) for dev in range(8)])]
    psum x1 -> x0, waiting for transfers between devices: 78.9 us -> none  [shards(): gram_matrix = lax.psum(local_gram, 'spec')]
    ppermute x0 -> x3, starting transfers between devices: none -> 6.11 us  [shards(): lax.ppermute(gram_matrix, 'spec', [(dev, dev ^ hop) for dev in range(8)])]
  transfers between devices with their start and end apart: 4 -> 6, of which waited for: 3 -> 5; matrix products, arithmetic and copies ran while one was open for 1% -> 1% of each run, Pallas kernels for 0% -> 0%
where the time goes in v1:
time: 248 us
  waiting for transfers between devices  124 us (50%)
  other arithmetic  85.7 us (35%)
  between operations  16.9 us (7%)
  starting transfers between devices  9.8 us (4%)
  matrix products  5.48 us (2%)
  local copies, waits for them, and re-layouts  5.46 us (2%)
    ppermute x3, waiting for transfers between devices, shards(): lax.ppermute(gram_matrix, 'spec', [(dev, dev ^ hop) for dev in range(8)])  86.4 us
    another operation x14, other arithmetic, shards(): rfactor = jnp.linalg.cholesky(gram_matrix).T  78.9 us
    psum x1, waiting for transfers between devices, shards(): sketch = lax.psum(partial_sketch, 'wave')  36.8 us
    ppermute x3, starting transfers between devices, shards(): lax.ppermute(gram_matrix, 'spec', [(dev, dev ^ hop) for dev in range(8)])  6.11 us
  transfers between devices with their start and end apart: 6, of which 5 were waited for; matrix products, arithmetic and copies ran while one was open for 1% of the time, Pallas kernels for 0%

profile of v1, /device:TPU:0, one launch (start us, length us, event | category | flops | bytes accessed | tf_op | source)
XLA Modules:
  0.0 247.8 jit_solution(3663417687345651099)
XLA Ops:
  7.2 0.7 convert_element_type.15
  8.0 0.8 select_reduce_fusion.1
  8.8 0.7 mul.59
  9.5 2.2 fusion.5
  11.8 2.4 collective-permute-start
  14.3 1.3 collective-permute-start.1
  16.0 0.6 compare_reduce_fusion.4
  16.6 0.7 add_select_fusion
  17.3 1.1 scatter-add.6
  18.4 1.3 collective-permute-done.1
  19.7 1.1 scatter-add.9
  21.1 1.1 fusion.19
  22.3 36.8 %all-reduce.3.cloned.1.call-done = f32[256,512]{1,0:T(8,128)} async-done(((f32[256,512]{1,0:T(8,128)}), f32[256,512]{1,0:T(8,128)}) %all-reduce.3.cloned.1.call-update) | async-done | bytes 524304 | tf_op jit(solution)/shard_map/psum | solution.py:77
  59.1 2.3 fusion.20
  61.4 1.5 collective-permute-start.2
  62.9 22.2 %collective-permute-done.2 = f32[512,512]{0,1:T(8,128)S(1)} collective-permute-done((f32[512,512]{0,1:T(8,128)S(1)}, f32[512,512]{0,1:T(8,128)S(1)}, u32[]{:S(2)}, u32[]{:S(2)}) %collective-permute-start.2) | collective-permute-done | bytes 1048608 | tf_op jit(solution)/shard_map/ppermute | solution.py:83
  85.3 1.8 collective-permute-start.3
  87.2 21.3 %collective-permute-done.3 = f32[512,512]{0,1:T(8,128)S(1)} collective-permute-done((f32[512,512]{0,1:T(8,128)S(1)}, f32[512,512]{0,1:T(8,128)S(1)}, u32[]{:S(2)}, u32[]{:S(2)}) %collective-permute-start.3) | collective-permute-done | bytes 1048608 | tf_op jit(solution)/shard_map/ppermute | solution.py:83
  108.7 2.8 %collective-permute-start.4 = (f32[512,512]{0,1:T(8,128)S(1)}, f32[512,512]{0,1:T(8,128)S(1)}, u32[]{:S(2)}, u32[]{:S(2)}) collective-permute-start(f32[512,512]{0,1:T(8,128)S(1)} %add.91), channel_id=1, source_target_pairs={{0,16},{4,20},{8,24},{12,28},{16,0},{20,4},{24,8},{28,12},{1,17},{... | collective-permute-start | bytes 3145736 | tf_op jit(solution)/shard_map/ppermute | solution.py:83
  111.4 42.8 %collective-permute-done.4 = f32[512,512]{0,1:T(8,128)S(1)} collective-permute-done((f32[512,512]{0,1:T(8,128)S(1)}, f32[512,512]{0,1:T(8,128)S(1)}, u32[]{:S(2)}, u32[]{:S(2)}) %collective-permute-start.4) | collective-permute-done | bytes 1048608 | tf_op jit(solution)/shard_map/ppermute | solution.py:83
  155.1 1.0 copy-done.1
  156.1 11.7 %cholesky.104 = f32[128,128]{1,0:T(8,128)S(1)} custom-call(f32[128,128]{1,0:T(8,128)S(1)} %cholesky.266), custom_call_target="Cholesky" | custom-call | tf_op jit(solution)/shard_map/jit(cholesky)/cholesky | solution.py:87
  167.8 9.8 %custom-call.27 = f32[1,128,128]{1,2,0:T(8,128)S(1)} custom-call(f32[1,128,128]{2,1,0:T(8,128)S(1)} %get-tuple-element.44), custom_call_target="InvertDiagBlocksLowerTriangular" | custom-call | tf_op jit(solution)/shard_map/jit(cholesky)/cholesky | solution.py:87
  178.4 11.9 %cholesky.217 = f32[128,128]{1,0:T(8,128)S(1)} custom-call(f32[128,128]{1,0:T(8,128)S(1)} %cholesky.270), custom_call_target="Cholesky" | custom-call | tf_op jit(solution)/shard_map/jit(cholesky)/cholesky | solution.py:87
  190.3 9.8 %custom-call.28 = f32[1,128,128]{1,2,0:T(8,128)S(1)} custom-call(f32[1,128,128]{2,1,0:T(8,128)S(1)} %get-tuple-element.41), custom_call_target="InvertDiagBlocksLowerTriangular" | custom-call | tf_op jit(solution)/shard_map/jit(cholesky)/cholesky | solution.py:87
  200.8 11.7 %cholesky.238 = f32[128,128]{1,0:T(8,128)S(1)} custom-call(f32[128,128]{1,0:T(8,128)S(1)} %cholesky.275), custom_call_target="Cholesky" | custom-call | tf_op jit(solution)/shard_map/jit(cholesky)/cholesky | solution.py:87
  212.6 0.7 compare_reduce_fusion.1
  213.3 9.8 %custom-call.29 = f32[1,128,128]{1,2,0:T(8,128)S(1)} custom-call(f32[1,128,128]{2,1,0:T(8,128)S(1)} %get-tuple-element.38), custom_call_target="InvertDiagBlocksLowerTriangular" | custom-call | tf_op jit(solution)/shard_map/jit(cholesky)/cholesky | solution.py:87
  223.7 12.0 %cholesky.255 = f32[128,128]{1,0:T(8,128)S(1)} custom-call(f32[128,128]{1,0:T(8,128)S(1)} %convolution_subtract_fusion.2), custom_call_target="Cholesky" | custom-call | tf_op jit(solution)/shard_map/jit(cholesky)/cholesky | solution.py:87
  235.7 0.6 compare_reduce_fusion
  236.3 0.7 compare_reduce_fusion.2
  239.7 1.3 copy.26
  (46 shorter events, 4.5 us)
Async XLA Ops:
  7.2 14.0 %copy-start = (bf16[512,512]{1,0:T(8,128)(2,1)S(1)}, bf16[512,512]{1,0:T(8,128)(2,1)}, u32[]{:S(2)}) copy-start(bf16[512,512]{1,0:T(8,128)(2,1)} %param.23) | copy-start | bytes 1572868
  7.2 51.9 %all-reduce.3.cloned.1.call-start = ((), (), s32[]{:S(2)}) async-start(), calls=%async_computation | async-start | bytes 1048576 | tf_op jit(solution)/shard_map/psum | solution.py:77
  11.8 4.8 %collective-permute-start = (f32[256,32]{1,0:T(8,128)S(1)}, f32[256,32]{1,0:T(8,128)S(1)}, u32[]{:S(2)}, u32[]{:S(2)}) collective-permute-start(f32[256,32]{1,0:T(8,128)S(1)} %copy.30), channel_id=1, source_target_pairs={{0,1},{1,2},{2,3},{4,5},{5,6},{6,7},{8,9},{9,10},{10,11},{12,13},{... | collective-permute-start | bytes 98312 | tf_op jit(solution)/shard_map/ppermute | solution.py:16
  14.3 5.3 %collective-permute-start.1 = (f32[256,32]{1,0:T(8,128)S(1)}, f32[256,32]{1,0:T(8,128)S(1)}, u32[]{:S(2)}, u32[]{:S(2)}) collective-permute-start(f32[256,32]{1,0:T(8,128)S(1)} %copy.31), channel_id=1, source_target_pairs={{1,0},{2,1},{3,2},{5,4},{6,5},{7,6},{9,8},{10,9},{11,10},{13,12},{... | collective-permute-start | bytes 98312 | tf_op jit(solution)/shard_map/ppermute | solution.py:19
  15.6 5.2 %copy-start.4 = (bf16[256,512]{1,0:T(8,128)(2,1)S(1)}, bf16[256,512]{1,0:T(8,128)(2,1)}, u32[]{:S(2)}) copy-start(bf16[256,512]{1,0:T(8,128)(2,1)} %param.14) | copy-start | bytes 786436
  15.7 5.2 %copy-start.5 = (bf16[16,512]{1,0:T(8,128)(2,1)S(1)}, bf16[16,512]{1,0:T(8,128)(2,1)}, u32[]{:S(2)}) copy-start(bf16[16,512]{1,0:T(8,128)(2,1)} %param.16) | copy-start | bytes 49156
  15.7 5.2 %copy-start.6 = (bf16[256,16]{0,1:T(8,128)(2,1)S(1)}, bf16[256,16]{0,1:T(8,128)(2,1)}, u32[]{:S(2)}) copy-start(bf16[256,16]{0,1:T(8,128)(2,1)} %param.15) | copy-start | bytes 24580
  21.1 40.2 %copy-start.3 = (bf16[256,512]{1,0:T(8,128)(2,1)}, bf16[256,512]{1,0:T(8,128)(2,1)S(1)}, u32[]{:S(2)}) copy-start(bf16[256,512]{1,0:T(8,128)(2,1)S(1)} %subtract_convert_fusion) | copy-start | bytes 786436
  61.4 23.8 %collective-permute-start.2 = (f32[512,512]{0,1:T(8,128)S(1)}, f32[512,512]{0,1:T(8,128)S(1)}, u32[]{:S(2)}, u32[]{:S(2)}) collective-permute-start(f32[512,512]{0,1:T(8,128)S(1)} %fusion.20), channel_id=1, source_target_pairs={{0,4},{4,0},{8,12},{12,8},{16,20},{20,16},{24,28},{28,24},{1,5},{5... | collective-permute-start | bytes 3145736 | tf_op jit(solution)/shard_map/ppermute | solution.py:83
  85.3 23.1 %collective-permute-start.3 = (f32[512,512]{0,1:T(8,128)S(1)}, f32[512,512]{0,1:T(8,128)S(1)}, u32[]{:S(2)}, u32[]{:S(2)}) collective-permute-start(f32[512,512]{0,1:T(8,128)S(1)} %add.90), channel_id=1, source_target_pairs={{0,8},{4,12},{8,0},{12,4},{16,24},{20,28},{24,16},{28,20},{1,9},{5... | collective-permute-start | bytes 3145736 | tf_op jit(solution)/shard_map/ppermute | solution.py:83
  108.7 45.6 %collective-permute-start.4 = (f32[512,512]{0,1:T(8,128)S(1)}, f32[512,512]{0,1:T(8,128)S(1)}, u32[]{:S(2)}, u32[]{:S(2)}) collective-permute-start(f32[512,512]{0,1:T(8,128)S(1)} %add.91), channel_id=1, source_target_pairs={{0,16},{4,20},{8,24},{12,28},{16,0},{20,4},{24,8},{28,12},{1,17},{... | collective-permute-start | bytes 3145736 | tf_op jit(solution)/shard_map/ppermute | solution.py:83
  155.1 1.0 copy-start.1
  156.0 21.7 %copy-start.2 = (f32[512,512]{1,0:T(8,128)S(1)}, f32[512,512]{1,0:T(8,128)}, u32[]{:S(2)}) copy-start(f32[512,512]{1,0:T(8,128)} %copy-done.1) | copy-start | bytes 3145732
Sparse Core Ops, SparseCore 0:
  22.4 36.6 all-reduce.2
